TPU v7x, 32 devices: a whole 2x2x4 slice. The times are simulated.
32 devices in a mesh: seq: 8 (over y, x, core), exp: 4 (over z).
Axes of the slice: x: 2, y: 2, z: 4, core: 2. Of those that a mesh axis runs over, the one named last changes fastest.
Arguments:
- queries: bfloat16 [1024, 2048], P('seq', 'exp'), may hold values from -10 to 10
- key_rows: bfloat16 [1024, 2048], P('seq', 'exp'), may hold values from -10 to 10
- value_rows: bfloat16 [1024, 2048], P('seq', 'exp'), may hold values from -6 to 6
- residual: bfloat16 [1024, 2048], P('seq'), may hold values from -20 to 20
- out_weight: bfloat16 [2048, 2048], P('exp'), may hold values from -1 to 1
- norm_gain: float32 [2048], replicated, may hold values from 0.5 to 1.5
- gate_weight: bfloat16 [16, 2048, 1408], P('seq', None, 'exp'), may hold values from -0.125 to 0.125
- up_weight: bfloat16 [16, 2048, 1408], P('seq', None, 'exp'), may hold values from -0.125 to 0.125
- down_weight: bfloat16 [16, 1408, 2048], P('seq', 'exp'), may hold values from -0.15625 to 0.15625
- routes: int32 [1024, 6], P('seq'), may hold values from 0 to 15, all different within a row; in each aligned block of 128 rows (0 to 127, 128 to 255, ...) at most 96 rows name the same one
- route_gates: float32 [1024, 6], P('seq'), may hold values from 0.2 to 1
- block_picks: int32 [2, 3], replicated, may hold values from 0 to 1, as said below
Outputs:
- layer_out: bfloat16 [1024, 2048], P(('seq', 'exp'))
Inputs may be any that keep to these rules, and one draw needn't show every extreme that they name: `block_picks`: row b names block b first, then blocks at or before b, repeats allowed. `routes`: in each aligned block of 128 rows no expert is named by more than 96 rows, a bound that some block reaches.
All inputs are finite; a program needn't handle non-finite values.
Results may differ from a plain program's by a relative error of at most 0.015.
Values may be sent and summed in bfloat16 or wider, within the bound.
No kernel may reach another device: no remote copies, remote signals or barrier semaphores. Data moves between devices by JAX's collectives and lax.ppermute only.
A program may use at most 64 MiB of HBM per device.

v0:
```python
import jax
import jax.numpy as jnp
from jax import lax
from jax.sharding import PartitionSpec as P

HD = 128
TOPK = 6
BLK = 512


def rms_scale(hidden, norm_gain):
    mean_square = jnp.mean(hidden * hidden, axis=-1, keepdims=True)
    return hidden * lax.rsqrt(mean_square + 1e-06) * norm_gain


def expert_block(arrived, gate_weight, up_weight, down_weight):
    gate_part = jnp.einsum(
        "semd,edf->semf", arrived, gate_weight, preferred_element_type=jnp.float32
    )
    up_part = jnp.einsum("semd,edf->semf", arrived, up_weight, preferred_element_type=jnp.float32)
    inner_act = (jax.nn.silu(gate_part) * up_part).astype(jnp.bfloat16)
    return jnp.einsum(
        "semf,efd->semd", inner_act, down_weight, preferred_element_type=jnp.float32
    ).astype(jnp.bfloat16)


def per_device(
    queries,
    key_rows,
    value_rows,
    residual,
    out_weight,
    norm_gain,
    gate_weight,
    up_weight,
    down_weight,
    routes,
    route_gates,
    block_picks,
):
    seq_count = lax.axis_size("seq")
    exp_count = lax.axis_size("exp")
    seq_index = lax.axis_index("seq")
    exp_index = lax.axis_index("exp")
    tok_rows = queries.shape[0]
    head_count = queries.shape[1] // HD
    nblocks = block_picks.shape[0]
    model_width = residual.shape[1]
    positions = seq_index * tok_rows + jnp.arange(tok_rows, dtype=jnp.int32)
    block_ids = jnp.arange(nblocks, dtype=jnp.int32)
    chosen = jnp.any(block_picks[:, :, None] == block_ids[None, None, :], axis=1).astype(
        jnp.float32
    )
    query_onehot = ((positions // BLK)[:, None] == block_ids[None, :]).astype(jnp.float32)
    query_allowed = jnp.dot(query_onehot, chosen)
    split_queries = queries.reshape(tok_rows, head_count, HD)
    score_scale = HD ** (-0.5)
    run_max = jnp.full((tok_rows, head_count), -1e30, jnp.float32)
    key_piece = lax.all_gather(key_rows, "seq", axis=0, tiled=True)
    value_piece = lax.all_gather(value_rows, "seq", axis=0, tiled=True)
    piece_rows = key_piece.shape[0]
    key_pos = jnp.arange(piece_rows, dtype=jnp.int32)
    key_onehot = ((key_pos // BLK)[:, None] == block_ids[None, :]).astype(jnp.float32)
    allowed = (
        (jnp.dot(query_allowed, key_onehot.T) > 0.5) & (key_pos[None, :] <= positions[:, None])
    )[:, None, :]
    scores = (
        jnp.einsum(
            "qhd,khd->qhk",
            split_queries,
            key_piece.reshape(piece_rows, head_count, HD),
            preferred_element_type=jnp.float32,
        )
        * score_scale
    )
    piece_max = jnp.max(jnp.where(allowed, scores, -1e30), axis=2)
    new_max = jnp.maximum(run_max, piece_max)
    expo = jnp.where(allowed, jnp.exp(scores - new_max[:, :, None]), 0.0)
    new_total = jnp.sum(expo, axis=2)
    mixed_values = jnp.einsum(
        "qhk,khd->qhd",
        expo.astype(jnp.bfloat16),
        value_piece.reshape(piece_rows, head_count, HD),
        preferred_element_type=jnp.float32,
    )
    attended = (
        (mixed_values / new_total[:, :, None])
        .astype(jnp.bfloat16)
        .reshape(tok_rows, head_count * HD)
    )
    proj_part = jnp.dot(attended, out_weight, preferred_element_type=jnp.float32)
    share_rows = tok_rows // exp_count
    projected = lax.psum_scatter(
        proj_part.astype(jnp.bfloat16), "exp", scatter_dimension=0, tiled=True
    ).astype(jnp.float32)
    own_residual = lax.dynamic_slice_in_dim(residual, exp_index * share_rows, share_rows, 0).astype(
        jnp.float32
    )
    own_hidden = own_residual + projected
    own_normed = rms_scale(own_hidden, norm_gain).astype(jnp.bfloat16)
    normed = lax.all_gather(own_normed, "exp", axis=0, tiled=True)
    local_experts = gate_weight.shape[0]
    expert_count = local_experts * seq_count
    slot_most = exp_count * max(1, 2 * tok_rows * TOPK // (expert_count * exp_count))
    slot_total = expert_count * slot_most
    pair_count = tok_rows * TOPK
    flat_routes = routes.reshape(pair_count)
    route_onehot = (
        flat_routes[:, None] == jnp.arange(expert_count, dtype=jnp.int32)[None, :]
    ).astype(jnp.int32)
    slot_rank = jnp.sum((jnp.cumsum(route_onehot, axis=0) - 1) * route_onehot, axis=1)
    slot_ids = flat_routes * slot_most + slot_rank
    sources = (
        jnp.full((slot_total,), pair_count, jnp.int32)
        .at[slot_ids]
        .set(jnp.arange(pair_count, dtype=jnp.int32))
    )
    live_slot = sources < pair_count
    token_ids = jnp.minimum(sources, pair_count - 1) // TOPK
    outgoing = jnp.where(live_slot[:, None], normed[token_ids], jnp.zeros((), jnp.bfloat16))
    outgoing = outgoing.reshape(seq_count, local_experts, slot_most, model_width)
    returned = lax.all_to_all(
        expert_block(
            lax.all_to_all(outgoing, "seq", split_axis=0, concat_axis=0, tiled=True),
            gate_weight,
            up_weight,
            down_weight,
        ),
        "seq",
        split_axis=0,
        concat_axis=0,
        tiled=True,
    )
    back_rows = returned.reshape(slot_total, model_width)[slot_ids].astype(jnp.float32)
    weighted = back_rows.reshape(tok_rows, TOPK, model_width) * route_gates[:, :, None]
    mixture_part = jnp.sum(weighted, axis=1)
    own_mixture = lax.psum_scatter(
        mixture_part.astype(jnp.bfloat16), "exp", scatter_dimension=0, tiled=True
    ).astype(jnp.float32)
    return (own_hidden + own_mixture).astype(jnp.bfloat16)


def solution(mesh):
    placed = (
        P("seq", "exp"),
        P("seq", "exp"),
        P("seq", "exp"),
        P("seq", None),
        P("exp", None),
        P(),
        P("seq", None, "exp"),
        P("seq", None, "exp"),
        P("seq", "exp", None),
        P("seq", None),
        P("seq", None),
        P(),
    )
    return jax.shard_map(
        per_device, mesh=mesh, in_specs=placed, out_specs=P(("seq", "exp"), None), check_vma=False
    )
```

profile of v0, /device:TPU:0, one launch (start us, length us, event | category | flops | bytes accessed | tf_op | source)
XLA Modules:
  0.0 345.7 jit_solution(12460206369254408509)
XLA Ops:
  6.5 1.8 copy.47
  8.4 0.0 all-gather.3.cloned.1.call-update
  8.4 0.0 all-gather.5.cloned.1.call-start
  8.4 0.7 all-gather.5.cloned.1.call-update
  9.1 0.0 reduce-scatter.3.cloned.1.call-start
  9.2 0.8 fusion.49
  10.0 0.6 fusion.27
  10.5 0.3 copy.46
  10.8 0.8 copy.53
  11.6 0.1 eq.77
  11.8 1.7 reduce-window.6
  13.5 22.0 %all-gather.3.cloned.1.call-done = bf16[1024,512]{0,1:T(8,128)(2,1)} async-done(((bf16[128,512]{0,1:T(8,128)(2,1)}), bf16[1024,512]{0,1:T(8,128)(2,1)}) %all-gather.3.cloned.1.call-update) | async-done | bytes 1048592 | tf_op jit(solution)/shard_map/all_gather | solution.py:59
  35.4 1.9 fusion.11
  37.3 1.3 copy-done.2
  38.7 0.5 fusion.22
  39.1 21.6 %all-gather.5.cloned.1.call-done = bf16[1024,512]{1,0:T(8,128)(2,1)} async-done(((bf16[128,512]{1,0:T(8,128)(2,1)}), bf16[1024,512]{1,0:T(8,128)(2,1)}) %all-gather.5.cloned.1.call-update) | async-done | bytes 1048592 | tf_op jit(solution)/shard_map/all_gather | solution.py:60
  60.7 2.3 copy.50
  63.0 2.7 fusion.26
  65.8 1.3 convolution_convert_fusion
  67.1 0.0 reduce-scatter.3.cloned.1.call-update
  67.1 0.2 slice_reduce_fusion
  67.3 0.1 eq.73
  67.5 0.1 copy.52
  67.6 0.1 mul.75
  67.8 0.1 fusion.40
  67.9 3.4 scatter_custom_fusion
  71.3 0.1 broadcast_in_dim.60
  71.4 17.6 %reduce-scatter.3.cloned.1.call-done = bf16[32,2048]{1,0:T(8,128)(2,1)} async-done(((bf16[128,2048]{1,0:T(8,128)(2,1)}), bf16[32,2048]{1,0:T(8,128)(2,1)}) %reduce-scatter.3.cloned.1.call-update) | async-done | bytes 131088 | tf_op jit(solution)/shard_map/reduce_scatter | solution.py:93
  89.1 1.1 multiply_reduce_fusion.1
  90.2 1.1 multiply_convert_fusion
  91.3 15.4 %all_gather.11 = bf16[128,2048]{1,0:T(8,128)(2,1)S(1)} all-gather(bf16[32,2048]{1,0:T(8,128)(2,1)S(1)} %multiply_convert_fusion), channel_id=1, replica_groups=mesh['seq'=8,'exp'=4] {'exp'}, dimensions={0}, use_global_device_ids=true | all-gather | bytes 655360 | tf_op jit(solution)/shard_map/all_gather | solution.py:101
  106.6 7.1 %gather_fusion = bf16[1536,2048]{1,0:T(8,128)(2,1)} fusion(bf16[128,2048]{1,0:T(8,128)(2,1)S(1)} %all_gather.11, s32[2048]{0:T(1024)S(1)} %pad_clamp_fusion), kind=kCustom, calls=%fused_computation | custom fusion | bytes 12589056 | tf_op jit(solution)/shard_map/gather | solution.py:120
  113.7 3.3 broadcast_select_fusion
  117.0 75.3 %all_to_all.10 = bf16[8,2,96,2048]{3,2,1,0:T(8,128)(2,1)S(1)} all-to-all(bf16[8,2,96,2048]{3,2,1,0:T(8,128)(2,1)S(1)} %broadcast_select_fusion), channel_id=1, replica_groups=mesh['seq'=8,'exp'=4] {'seq'}, dimensions={0} | all-to-all | bytes 12582912 | tf_op jit(solution)/shard_map/all_to_all | solution.py:124
  192.4 2.7 copy-done.3
  195.0 4.8 %fusion.2 = f32[2,8,96,352]{3,2,1,0:T(8,128)} fusion(bf16[8,2,96,2048]{3,2,1,0:T(8,128)(2,1)S(1)} %all_to_all.10, bf16[2,2048,352]{1,2,0:T(8,128)(2,1)S(1)} %copy-done.9), kind=kOutput, calls=%fused_computation.8 | convolution fusion | flops 2214592512 | bytes 11337728 | tf_op jit(solution)/shard_map/semd,edf->semf/dot_general | solution.py:17
  199.9 11.2 %convert_bitcast_fusion = bf16[8,2,96,2048]{3,2,0,1:T(8,128)(2,1)} fusion(bf16[2,352,2048]{2,1,0:T(8,128)(2,1)S(1)} %copy-done, f32[2,8,96,352]{3,2,1,0:T(8,128)} %fusion.2, bf16[2,2048,352]{1,2,0:T(8,128)(2,1)} %param.19, bf16[8,2,96,2048]{3,2,1,0:T(8,128)(2,1)} %copy-done.3), kind=kOutput, calls=%fused_computation.4 | convolution fusion | flops 4435574784 | bytes 20512768 | tf_op jit(solution)/shard_map/semf,efd->semd/dot_general | solution.py:22
  211.1 6.6 %copy.58 = bf16[8,2,96,2048]{3,2,1,0:T(8,128)(2,1)} copy(bf16[8,2,96,2048]{3,2,0,1:T(8,128)(2,1)} %convert_bitcast_fusion) | data formatting | bytes 12582912 | tf_op jit(solution)/shard_map/convert_element_type | solution.py:24
  217.7 4.9 %all-to-all-start.1 = ((bf16[8,2,96,2048]{3,2,1,0:T(8,128)(2,1)}), bf16[8,2,96,2048]{3,2,1,0:T(8,128)(2,1)}, u32[]{:S(2)}, u32[]{:S(2)}) async-start(bf16[8,2,96,2048]{3,2,1,0:T(8,128)(2,1)} %copy.58), calls=%async_computation.2 | async-start | bytes 12582912 | tf_op jit(solution)/shard_map/all_to_all | solution.py:122
  222.6 0.3 reduce-scatter.5.cloned.1.call-start
  222.8 0.1 copy.59
  223.0 71.2 %all-to-all-done.1 = bf16[8,2,96,2048]{3,2,1,0:T(8,128)(2,1)} async-done(((bf16[8,2,96,2048]{3,2,1,0:T(8,128)(2,1)}), bf16[8,2,96,2048]{3,2,1,0:T(8,128)(2,1)}, u32[]{:S(2)}, u32[]{:S(2)}) %all-to-all-start.1) | async-done | bytes 6291488 | tf_op jit(solution)/shard_map/all_to_all | solution.py:122
  294.1 10.7 %gather_fusion.1 = bf16[768,2048]{1,0:T(8,128)(2,1)} fusion(bf16[1536,2048]{1,0:T(8,128)(2,1)} %bitcast.16, s32[1024]{0:T(1024)S(1)} %pad_clamp_fusion.1), kind=kCustom, calls=%fused_computation.1 | custom fusion | bytes 6294528 | tf_op jit(solution)/shard_map/gather | solution.py:134
  304.8 6.7 %reshape.131 = f32[128,6,2048]{2,1,0:T(8,128)} reshape(bf16[768,2048]{1,0:T(8,128)(2,1)} %gather_fusion.1) | data formatting | bytes 9437184 | tf_op jit(solution)/shard_map/convert_element_type | solution.py:134
  311.5 7.4 %multiply_reduce_fusion = bf16[128,2048]{1,0:T(8,128)(2,1)} fusion(f32[128,6,2048]{2,1,0:T(8,128)} %reshape.131, f32[128,6]{1,0:T(8,128)S(1)} %copy.59), kind=kLoop, calls=%fused_computation.3 | loop fusion | flops 2883584 | bytes 6818816 | tf_op jit(solution)/shard_map/reduce_sum | solution.py:136
  319.0 0.0 reduce-scatter.5.cloned.1.call-update
  319.0 18.5 %reduce-scatter.5.cloned.1.call-done = bf16[32,2048]{1,0:T(8,128)(2,1)} async-done(((bf16[128,2048]{1,0:T(8,128)(2,1)}), bf16[32,2048]{1,0:T(8,128)(2,1)}) %reduce-scatter.5.cloned.1.call-update) | async-done | bytes 131088 | tf_op jit(solution)/shard_map/reduce_scatter | solution.py:137
  337.5 1.7 add_convert_fusion
  (32 shorter events, 0.2 us)
Async XLA Ops:
  6.5 193.3 %copy-start = (bf16[2,352,2048]{2,1,0:T(8,128)(2,1)S(1)}, bf16[2,352,2048]{2,1,0:T(8,128)(2,1)}, u32[]{:S(2)}) copy-start(bf16[2,352,2048]{2,1,0:T(8,128)(2,1)} %param.20) | copy-start | bytes 8650756
  6.5 28.9 %all-gather.3.cloned.1.call-start = ((), (), s32[]{:S(2)}) async-start(), calls=%async_computation.4 | async-start | bytes 1179648 | tf_op jit(solution)/shard_map/all_gather | solution.py:59
  8.4 52.4 %all-gather.5.cloned.1.call-start = ((), (), s32[]{:S(2)}) async-start(), calls=%async_computation.5 | async-start | bytes 1179648 | tf_op jit(solution)/shard_map/all_gather | solution.py:60
  9.1 79.9 %reduce-scatter.3.cloned.1.call-start = ((), (), s32[]{:S(2)}) async-start(), calls=%async_computation.6 | async-start | bytes 655360 | tf_op jit(solution)/shard_map/reduce_scatter | solution.py:93
  37.3 1.4 copy-start.2
  63.0 2.8 copy-start.4
  65.8 1.7 copy-start.6
  65.8 24.4 %copy-start.7 = (f32[2048]{0:T(1024)S(1)}, f32[2048]{0:T(1024)}, u32[]{:S(2)}) copy-start(f32[2048]{0:T(1024)} %param.17) | copy-start | bytes 24580
  117.0 78.0 %copy-start.9 = (bf16[2,2048,352]{1,2,0:T(8,128)(2,1)S(1)}, bf16[2,2048,352]{1,2,0:T(8,128)(2,1)}, u32[]{:S(2)}) copy-start(bf16[2,2048,352]{1,2,0:T(8,128)(2,1)} %param.18) | copy-start | bytes 8650756
  192.4 2.7 copy-start.3
  217.7 5.2 %copy-start.8 = (f32[128,6]{0,1:T(8,128)S(1)}, f32[128,6]{0,1:T(8,128)}, u32[]{:S(2)}) copy-start(f32[128,6]{0,1:T(8,128)} %param.22) | copy-start | bytes 9220
  217.7 76.4 %all-to-all-start.1 = ((bf16[8,2,96,2048]{3,2,1,0:T(8,128)(2,1)}), bf16[8,2,96,2048]{3,2,1,0:T(8,128)(2,1)}, u32[]{:S(2)}, u32[]{:S(2)}) async-start(bf16[8,2,96,2048]{3,2,1,0:T(8,128)(2,1)} %copy.58), calls=%async_computation.2 | async-start | bytes 12582912 | tf_op jit(solution)/shard_map/all_to_all | solution.py:122
  222.6 115.0 %reduce-scatter.5.cloned.1.call-start = ((), (), s32[]{:S(2)}) async-start(), calls=%async_computation.7 | async-start | bytes 655360 | tf_op jit(solution)/shard_map/reduce_scatter | solution.py:137
  304.8 34.4 %copy-start.1 = (bf16[2,352,2048]{2,1,0:T(8,128)(2,1)S(1)}, bf16[2,352,2048]{2,1,0:T(8,128)(2,1)}, u32[]{:S(2)}) copy-start(bf16[2,352,2048]{2,1,0:T(8,128)(2,1)} %param.20) | copy-start | bytes 8650756
  311.5 26.0 %copy-start.5 = (bf16[32,2048]{1,0:T(8,128)(2,1)S(1)}, bf16[32,2048]{1,0:T(8,128)(2,1)}, u32[]{:S(2)}) copy-start(bf16[32,2048]{1,0:T(8,128)(2,1)} %reduce-scatter.3.cloned.1.call-done) | copy-start | bytes 393220
Sparse Core Ops, SparseCore 0:
  9.2 26.1 all-gather.2
  37.3 23.3 all-gather.4
  67.2 21.8 reduce-scatter.2
  319.1 18.3 reduce-scatter.4
where the time goes:
time: 346 us
  waiting for transfers between devices  152 us (44%)
  blocking collectives  90.7 us (26%)
  local copies, waits for them, and re-layouts  44.6 us (13%)
  matrix products  22.5 us (7%)
  other arithmetic  17.8 us (5%)
  between operations  13.3 us (4%)
  starting transfers between devices  5.21 us (2%)
    all_to_all x1, blocking collectives, per_device(): lax.all_to_all(outgoing, 'seq', split_axis=0, concat_axis=0, tiled=True)  75.3 us
    all_to_all x1, waiting for transfers between devices, per_device(): lax.all_to_all(expert_block(lax.all_to_all(outgoing, 'seq', split_axis=0,...  71.2 us
    all_gather x1, waiting for transfers between devices, per_device(): key_piece = lax.all_gather(key_rows, 'seq', axis=0, tiled=True)  22 us
    all_gather x1, waiting for transfers between devices, per_device(): value_piece = lax.all_gather(value_rows, 'seq', axis=0, tiled=True)  21.6 us
    reduce_scatter x1, waiting for transfers between devices, per_device(): lax.psum_scatter(mixture_part.astype(jnp.bfloat16), 'exp', scatter_dimens...  18.5 us
    reduce_scatter x1, waiting for transfers between devices, per_device(): lax.psum_scatter(proj_part.astype(jnp.bfloat16), 'exp', scatter_dimension...  17.6 us
    all_gather x1, blocking collectives, per_device(): normed = lax.all_gather(own_normed, 'exp', axis=0, tiled=True)  15.4 us
    dot_general x1, matrix products, expert_block(): jnp.einsum('semf,efd->semd', inner_act, down_weight, preferred_element_ty...  11.2 us
  transfers between devices with their start and end apart: 5, of which 5 were waited for; matrix products, arithmetic and copies ran while one was open for 3% of the time, Pallas kernels for 0%

commit v1 on v0

--- a/solution.py
+++ b/solution.py
@@ -56,7 +56,21 @@
     split_queries = queries.reshape(tok_rows, head_count, HD)
     score_scale = HD ** (-0.5)
     run_max = jnp.full((tok_rows, head_count), -1e30, jnp.float32)
-    key_piece = lax.all_gather(key_rows, "seq", axis=0, tiled=True)
+
+    def _do_slots(s0, named_axis="seq"):
+        m_next, step_out = (jax.lax.axis_size(named_axis), jax.lax.axis_index(named_axis))
+        upper, high = (s0, 1)
+        while high < m_next:
+            work_now = jax.lax.ppermute(
+                upper, axis_name=named_axis, perm=[(ii, ii ^ high) for ii in range(m_next)]
+            )
+            piece_out = jnp.concatenate([upper, work_now], axis=0)
+            answer = jnp.concatenate([work_now, upper], axis=0)
+            upper = jnp.where(step_out & high == 0, piece_out, answer)
+            high = 2 * high
+        return upper
+
+    key_piece = _do_slots(key_rows)
     value_piece = lax.all_gather(value_rows, "seq", axis=0, tiled=True)
     piece_rows = key_piece.shape[0]
     key_pos = jnp.arange(piece_rows, dtype=jnp.int32)

time: 346 us -> 327 us (0.945)
  waiting for transfers between devices: 152 us -> 122 us
  starting transfers between devices: 5.21 us -> 9.97 us
  other arithmetic: 17.8 us -> 21.4 us
    all_gather x1 -> x0, waiting for transfers between devices: 22 us -> none  [per_device(): key_piece = lax.all_gather(key_rows, 'seq', axis=0, tiled=True)]
    all_gather x1, waiting for transfers between devices: 21.6 us -> 0.02 us  [per_device(): value_piece = lax.all_gather(value_rows, 'seq', axis=0, tiled=True)]
    ppermute x0 -> x3, waiting for transfers between devices: none -> 13.8 us  [_do_slots(): jax.lax.ppermute(upper, axis_name=named_axis, perm=[(ii, ii ^ high) for i...]
    ppermute x0 -> x3, starting transfers between devices: none -> 4.79 us  [_do_slots(): jax.lax.ppermute(upper, axis_name=named_axis, perm=[(ii, ii ^ high) for i...]
  transfers between devices with their start and end apart: 5 -> 7, of which waited for: 5 -> 5; matrix products, arithmetic and copies ran while one was open for 3% -> 5% of each run, Pallas kernels for 0% -> 0%
where the time goes in v1:
time: 327 us; the launch traced here: 326 us
  waiting for transfers between devices  122 us (37%)
  blocking collectives  90.7 us (28%)
  local copies, waits for them, and re-layouts  46.8 us (14%)
  matrix products  21.9 us (7%)
  other arithmetic  21.4 us (7%)
  between operations  13.4 us (4%)
  starting transfers between devices  9.97 us (3%)
    all_to_all x1, blocking collectives, per_device(): lax.all_to_all(outgoing, 'seq', split_axis=0, concat_axis=0, tiled=True)  75.3 us
    all_to_all x1, waiting for transfers between devices, per_device(): lax.all_to_all(expert_block(lax.all_to_all(outgoing, 'seq', split_axis=0,...  71.2 us
    reduce_scatter x1, waiting for transfers between devices, per_device(): lax.psum_scatter(mixture_part.astype(jnp.bfloat16), 'exp', scatter_dimens...  18.5 us
    reduce_scatter x1, waiting for transfers between devices, per_device(): lax.psum_scatter(proj_part.astype(jnp.bfloat16), 'exp', scatter_dimension...  18.3 us
    all_gather x1, blocking collectives, per_device(): normed = lax.all_gather(own_normed, 'exp', axis=0, tiled=True)  15.4 us
    ppermute x3, waiting for transfers between devices, _do_slots(): jax.lax.ppermute(upper, axis_name=named_axis, perm=[(ii, ii ^ high) for i...  13.8 us
    dot_general x1, matrix products, expert_block(): jnp.einsum('semf,efd->semd', inner_act, down_weight, preferred_element_ty...  11.2 us
    gather x1, local copies, waits for them, and re-layouts, per_device(): returned.reshape(slot_total, model_width)[slot_ids].astype(jnp.float32)  10.7 us
  transfers between devices with their start and end apart: 7, of which 5 were waited for; matrix products, arithmetic and copies ran while one was open for 5% of the time, Pallas kernels for 0%

profile of v1, /device:TPU:0, one launch (start us, length us, event | category | flops | bytes accessed | tf_op | source)
XLA Modules:
  0.0 326.2 jit_solution(11906393414688956472)
XLA Ops:
  6.5 0.5 collective-permute-start
  7.0 0.2 all-gather.2.cloned.1.call-update
  7.3 0.8 fusion.55
  8.2 0.8 copy.79
  9.0 0.1 eq.89
  9.1 1.2 fusion.27
  10.3 0.6 copy-done.6
  11.0 1.0 maximum_select_fusion.5
  12.0 3.0 collective-permute-start.1
  15.1 0.6 fusion.47
  15.7 1.8 copy.66
  17.4 3.2 reduce-window.6
  20.6 1.0 copy_bitcast_fusion.3
  21.6 0.4 collective-permute-done.1
  22.0 0.2 maximum_select_fusion.3
  22.3 1.3 collective-permute-start.2
  23.5 0.9 copy_bitcast_fusion.2
  24.6 0.1 maximum_select_fusion.2
  24.7 13.4 %collective-permute-done.2 = bf16[512,512]{1,0:T(8,128)(2,1)S(1)} collective-permute-done((bf16[512,512]{1,0:T(8,128)(2,1)S(1)}, bf16[512,512]{1,0:T(8,128)(2,1)S(1)}, u32[]{:S(2)}, u32[]{:S(2)}) %collective-permute-start.2) | collective-permute-done | bytes 524320 | tf_op jit(solution)/shard_map/ppermute | solution.py:64
  38.2 0.6 fusion.11
  38.9 1.3 copy-done.4
  40.2 0.5 fusion.22
  40.7 2.3 copy.76
  43.0 2.7 fusion.26
  45.8 1.3 convolution_convert_fusion
  47.1 0.2 slice_reduce_fusion
  47.3 0.1 eq.85
  47.6 0.1 mul.75
  47.9 3.4 %scatter_custom_fusion = s32[1536]{0:T(1024)S(1)} fusion(s32[768]{0:T(1024)S(1)} %fusion.57, s32[768]{0:T(1024)S(1)} %iota.36, s32[]{:T(128)} %constant.85.clone.1), kind=kCustom, calls=%fused_computation.89 | custom fusion | bytes 6148 | tf_op jit(solution)/shard_map/scatter | solution.py:130
  51.4 18.3 %reduce-scatter.3.cloned.1.call-done = bf16[32,2048]{1,0:T(8,128)(2,1)} async-done(((bf16[128,2048]{1,0:T(8,128)(2,1)}), bf16[32,2048]{1,0:T(8,128)(2,1)}) %reduce-scatter.3.cloned.1.call-update) | async-done | bytes 131088 | tf_op jit(solution)/shard_map/reduce_scatter | solution.py:107
  69.7 1.1 multiply_reduce_fusion.1
  70.8 1.0 multiply_convert_fusion
  71.8 15.4 %all_gather.7 = bf16[128,2048]{1,0:T(8,128)(2,1)S(1)} all-gather(bf16[32,2048]{1,0:T(8,128)(2,1)S(1)} %multiply_convert_fusion), channel_id=1, replica_groups=mesh['seq'=8,'exp'=4] {'exp'}, dimensions={0}, use_global_device_ids=true | all-gather | bytes 655360 | tf_op jit(solution)/shard_map/all_gather | solution.py:115
  87.1 7.1 %gather_fusion = bf16[1536,2048]{1,0:T(8,128)(2,1)} fusion(bf16[128,2048]{1,0:T(8,128)(2,1)S(1)} %all_gather.7, s32[2048]{0:T(1024)S(1)} %pad_clamp_fusion), kind=kCustom, calls=%fused_computation | custom fusion | bytes 12589056 | tf_op jit(solution)/shard_map/gather | solution.py:134
  94.2 3.3 %broadcast_select_fusion = bf16[8,2,96,2048]{3,2,1,0:T(8,128)(2,1)S(1)} fusion(bf16[8,2,96,2048]{3,2,1,0:T(8,128)(2,1)} %bitcast.115, pred[8,2,96]{2,1,0:T(4,128)(4,1)S(1)} %broadcast_in_dim.60), kind=kLoop, calls=%fused_computation.5 | loop fusion | flops 3145728 | bytes 12584448 | tf_op jit(solution)/shard_map/jit(_where)/select_n | solution.py:134
  97.5 75.3 %all_to_all.10 = bf16[8,2,96,2048]{3,2,1,0:T(8,128)(2,1)S(1)} all-to-all(bf16[8,2,96,2048]{3,2,1,0:T(8,128)(2,1)S(1)} %broadcast_select_fusion), channel_id=1, replica_groups=mesh['seq'=8,'exp'=4] {'seq'}, dimensions={0} | all-to-all | bytes 12582912 | tf_op jit(solution)/shard_map/all_to_all | solution.py:138
  172.9 2.7 copy-done.2
  175.5 4.8 %fusion.2 = f32[2,8,96,352]{3,2,1,0:T(8,128)} fusion(bf16[8,2,96,2048]{3,2,1,0:T(8,128)(2,1)S(1)} %all_to_all.10, bf16[2,2048,352]{1,2,0:T(8,128)(2,1)S(1)} %copy-done.13), kind=kOutput, calls=%fused_computation.8 | convolution fusion | flops 2214592512 | bytes 11337728 | tf_op jit(solution)/shard_map/semd,edf->semf/dot_general | solution.py:17
  180.4 11.2 %convert_bitcast_fusion = bf16[8,2,96,2048]{3,2,0,1:T(8,128)(2,1)} fusion(bf16[2,352,2048]{2,1,0:T(8,128)(2,1)S(1)} %copy-done, f32[2,8,96,352]{3,2,1,0:T(8,128)} %fusion.2, bf16[2,2048,352]{1,2,0:T(8,128)(2,1)} %param.19, bf16[8,2,96,2048]{3,2,1,0:T(8,128)(2,1)} %copy-done.2), kind=kOutput, calls=%fused_computation.4 | convolution fusion | flops 4435574784 | bytes 20512768 | tf_op jit(solution)/shard_map/semf,efd->semd/dot_general | solution.py:22
  191.6 6.6 %copy.84 = bf16[8,2,96,2048]{3,2,1,0:T(8,128)(2,1)} copy(bf16[8,2,96,2048]{3,2,0,1:T(8,128)(2,1)} %convert_bitcast_fusion) | data formatting | bytes 12582912 | tf_op jit(solution)/shard_map/convert_element_type | solution.py:24
  198.2 4.9 %all-to-all-start.1 = ((bf16[8,2,96,2048]{3,2,1,0:T(8,128)(2,1)}), bf16[8,2,96,2048]{3,2,1,0:T(8,128)(2,1)}, u32[]{:S(2)}, u32[]{:S(2)}) async-start(bf16[8,2,96,2048]{3,2,1,0:T(8,128)(2,1)} %copy.84), calls=%async_computation.2 | async-start | bytes 12582912 | tf_op jit(solution)/shard_map/all_to_all | solution.py:136
  203.1 0.3 reduce-scatter.5.cloned.1.call-start
  203.5 71.2 %all-to-all-done.1 = bf16[8,2,96,2048]{3,2,1,0:T(8,128)(2,1)} async-done(((bf16[8,2,96,2048]{3,2,1,0:T(8,128)(2,1)}), bf16[8,2,96,2048]{3,2,1,0:T(8,128)(2,1)}, u32[]{:S(2)}, u32[]{:S(2)}) %all-to-all-start.1) | async-done | bytes 6291488 | tf_op jit(solution)/shard_map/all_to_all | solution.py:136
  274.6 10.7 %gather_fusion.1 = bf16[768,2048]{1,0:T(8,128)(2,1)} fusion(bf16[1536,2048]{1,0:T(8,128)(2,1)} %bitcast.15, s32[1024]{0:T(1024)S(1)} %pad_clamp_fusion.1), kind=kCustom, calls=%fused_computation.1 | custom fusion | bytes 6294528 | tf_op jit(solution)/shard_map/gather | solution.py:148
  285.3 6.6 %reshape.140 = f32[128,6,2048]{2,1,0:T(8,128)} reshape(bf16[768,2048]{1,0:T(8,128)(2,1)} %gather_fusion.1) | data formatting | bytes 9437184 | tf_op jit(solution)/shard_map/convert_element_type | solution.py:148
  291.9 7.6 %multiply_reduce_fusion = bf16[128,2048]{1,0:T(8,128)(2,1)} fusion(f32[128,6,2048]{2,1,0:T(8,128)} %reshape.140, f32[128,6]{1,0:T(8,128)S(1)} %copy.85), kind=kLoop, calls=%fused_computation.3 | loop fusion | flops 2883584 | bytes 6818816 | tf_op jit(solution)/shard_map/reduce_sum | solution.py:150
  299.5 18.5 %reduce-scatter.5.cloned.1.call-done = bf16[32,2048]{1,0:T(8,128)(2,1)} async-done(((bf16[128,2048]{1,0:T(8,128)(2,1)}), bf16[32,2048]{1,0:T(8,128)(2,1)}) %reduce-scatter.5.cloned.1.call-update) | async-done | bytes 131088 | tf_op jit(solution)/shard_map/reduce_scatter | solution.py:151
  318.0 1.7 add_convert_fusion
  (52 shorter events, 0.9 us)
Async XLA Ops:
  6.5 173.8 %copy-start = (bf16[2,352,2048]{2,1,0:T(8,128)(2,1)S(1)}, bf16[2,352,2048]{2,1,0:T(8,128)(2,1)}, u32[]{:S(2)}) copy-start(bf16[2,352,2048]{2,1,0:T(8,128)(2,1)} %param.20) | copy-start | bytes 8650756
  6.5 34.2 %all-gather.2.cloned.1.call-start = ((), (), s32[]{:S(2)}) async-start(), calls=%async_computation.4 | async-start | bytes 1179648 | tf_op jit(solution)/shard_map/all_gather | solution.py:74
  6.5 3.8 %collective-permute-start = (bf16[128,512]{1,0:T(8,128)(2,1)}, bf16[128,512]{1,0:T(8,128)(2,1)S(1)}, u32[]{:S(2)}, u32[]{:S(2)}) collective-permute-start(bf16[128,512]{1,0:T(8,128)(2,1)} %param.13), channel_id=1, source_target_pairs={{0,4},{4,0},{8,12},{12,8},{16,20},{20,16},{24,28},{28,24},{1,5},{5... | collective-permute-start | bytes 393224 | tf_op jit(solution)/shard_map/ppermute | solution.py:64
  7.3 62.4 %reduce-scatter.3.cloned.1.call-start = ((), (), s32[]{:S(2)}) async-start(), calls=%async_computation.5 | async-start | bytes 655360 | tf_op jit(solution)/shard_map/reduce_scatter | solution.py:107
  10.3 0.6 copy-start.6
  12.0 10.0 %collective-permute-start.1 = (bf16[256,512]{1,0:T(8,128)(2,1)S(1)}, bf16[256,512]{1,0:T(8,128)(2,1)S(1)}, u32[]{:S(2)}, u32[]{:S(2)}) collective-permute-start(bf16[256,512]{1,0:T(8,128)(2,1)S(1)} %maximum_select_fusion.5), channel_id=1, source_target_pairs={{0,8},{4,12},{8,0},{12,4},{16,24},{20,28},{24,16},{28,20},{1,9},{5... | collective-permute-start | bytes 786440 | tf_op jit(solution)/shard_map/ppermute | solution.py:64
  20.6 17.6 %copy-start.7 = (pred[128,1024]{0,1:T(8,128)(4,1)S(1)}, pred[128,1024]{0,1:T(8,128)(4,1)}, u32[]{:S(2)}) copy-start(pred[128,1024]{0,1:T(8,128)(4,1)} %copy.66) | copy-start | bytes 393220
  20.6 17.6 %copy-start.14 = (bf16[128,512]{1,0:T(8,128)(2,1)S(1)}, bf16[128,512]{1,0:T(8,128)(2,1)}, u32[]{:S(2)}) copy-start(bf16[128,512]{1,0:T(8,128)(2,1)} %param.12) | copy-start | bytes 393220
  22.3 15.9 %collective-permute-start.2 = (bf16[512,512]{1,0:T(8,128)(2,1)S(1)}, bf16[512,512]{1,0:T(8,128)(2,1)S(1)}, u32[]{:S(2)}, u32[]{:S(2)}) collective-permute-start(bf16[512,512]{1,0:T(8,128)(2,1)S(1)} %maximum_select_fusion.3), channel_id=1, source_target_pairs={{0,16},{4,20},{8,24},{12,28},{16,0},{20,4},{24,8},{28,12},{1,17},{... | collective-permute-start | bytes 1572872 | tf_op jit(solution)/shard_map/ppermute | solution.py:64
  38.9 1.4 copy-start.4
  38.9 4.1 %copy-start.8 = (pred[128,1024]{0,1:T(8,128)(4,1)S(1)}, pred[128,1024]{0,1:T(8,128)(4,1)}, u32[]{:S(2)}) copy-start(pred[128,1024]{0,1:T(8,128)(4,1)} %copy.66) | copy-start | bytes 393220
  43.0 2.8 copy-start.3
  45.7 1.8 copy-start.10
  45.8 23.9 %copy-start.9 = (bf16[128,2048]{1,0:T(8,128)(2,1)S(1)}, bf16[128,2048]{1,0:T(8,128)(2,1)}, u32[]{:S(2)}) copy-start(bf16[128,2048]{1,0:T(8,128)(2,1)} %param.15) | copy-start | bytes 1572868
  45.8 25.0 %copy-start.11 = (f32[2048]{0:T(1024)S(1)}, f32[2048]{0:T(1024)}, u32[]{:S(2)}) copy-start(f32[2048]{0:T(1024)} %param.17) | copy-start | bytes 24580
  97.5 78.0 %copy-start.13 = (bf16[2,2048,352]{1,2,0:T(8,128)(2,1)S(1)}, bf16[2,2048,352]{1,2,0:T(8,128)(2,1)}, u32[]{:S(2)}) copy-start(bf16[2,2048,352]{1,2,0:T(8,128)(2,1)} %param.18) | copy-start | bytes 8650756
  172.9 2.7 copy-start.2
  198.2 5.2 %copy-start.12 = (f32[128,6]{0,1:T(8,128)S(1)}, f32[128,6]{0,1:T(8,128)}, u32[]{:S(2)}) copy-start(f32[128,6]{0,1:T(8,128)} %param.22) | copy-start | bytes 9220
  198.2 76.4 %all-to-all-start.1 = ((bf16[8,2,96,2048]{3,2,1,0:T(8,128)(2,1)}), bf16[8,2,96,2048]{3,2,1,0:T(8,128)(2,1)}, u32[]{:S(2)}, u32[]{:S(2)}) async-start(bf16[8,2,96,2048]{3,2,1,0:T(8,128)(2,1)} %copy.84), calls=%async_computation.2 | async-start | bytes 12582912 | tf_op jit(solution)/shard_map/all_to_all | solution.py:136
  203.1 114.9 %reduce-scatter.5.cloned.1.call-start = ((), (), s32[]{:S(2)}) async-start(), calls=%async_computation.6 | async-start | bytes 655360 | tf_op jit(solution)/shard_map/reduce_scatter | solution.py:151
  291.9 26.1 %copy-start.5 = (bf16[32,2048]{1,0:T(8,128)(2,1)S(1)}, bf16[32,2048]{1,0:T(8,128)(2,1)}, u32[]{:S(2)}) copy-start(bf16[32,2048]{1,0:T(8,128)(2,1)} %reduce-scatter.3.cloned.1.call-done) | copy-start | bytes 393220
  291.9 27.8 %copy-start.1 = (bf16[2,352,2048]{2,1,0:T(8,128)(2,1)S(1)}, bf16[2,352,2048]{2,1,0:T(8,128)(2,1)}, u32[]{:S(2)}) copy-start(bf16[2,352,2048]{2,1,0:T(8,128)(2,1)} %param.20) | copy-start | bytes 8650756
Sparse Core Ops, SparseCore 0:
  9.2 29.1 all-gather.1
  47.2 22.4 reduce-scatter.2
  299.6 18.3 reduce-scatter.4
